TPU v7x, 32 devices: a whole 2x2x4 slice. The times are simulated.
32 devices in a mesh: parts: 2 (over x), space: 16 (over z, y, core).
Axes of the slice: x: 2, y: 2, z: 4, core: 2. Of those that a mesh axis runs over, the one named last changes fastest.
Arguments:
- observed: bfloat16 [128, 4096, 128], P(('parts', 'space')), parts along dimension 0, may hold values from -6 to 6
- weights: bfloat16 [128, 4096, 128], P(('parts', 'space')), parts along dimension 0, may hold values from 0 to 1, as said below
- pixel_factors: float32 [128, 16, 4096], P(('parts', 'space')), parts along dimension 0, may hold values from -6 to 6
- pixel_bias: float32 [128, 4096], P(('parts', 'space')), parts along dimension 0, may hold values from -4 to 4
- date_factors: float32 [32, 128], P('parts'), parts along dimension 0, may hold values from -1.5 to 1.5
- date_bias: float32 [256], P('parts'), parts along dimension 0, may hold values from -4 to 4
- land_class: int32 [128, 4096], P(('parts', 'space')), parts along dimension 0, may hold values from 0 to 3
- conductance: float32 [4], replicated, may hold values from 0.3 to 3
Outputs:
- grad_pixel_factors: float32 [128, 16, 4096], P(('parts', 'space')), parts along dimension 0
- grad_pixel_bias: float32 [128, 4096], P(('parts', 'space')), parts along dimension 0
- grad_date_factors: float32 [32, 128], P('parts'), parts along dimension 0
- grad_date_bias: float32 [256], P('parts'), parts along dimension 0
There are 2 independent parts, one for each index of `parts`. A program takes and returns all parts, laid end to end along the dimension named above; an argument that names none is the same for every part. Nothing has to cross between parts.
Inputs may be any that keep to these rules, and one draw needn't show every extreme that they name: Every pixel has a nonzero weight on at least one date; nonzero weights are 0.5 or more.
All inputs are finite; a program needn't handle non-finite values.
Results may differ from a plain program's by a relative error of at most 0.0003.
Values sent between devices are 32-bit elements; how exact they have to be, the bound alone decides.
A program may use at most 64 MiB of HBM per device.

v0:
```python
import jax
import jax.numpy as jnp
from jax import lax
from jax.sharding import PartitionSpec as P

CLASSES = 4


def extended(block, sides, width):
    for axis, dim in sides:
        count = lax.axis_size(axis)
        forward = [(i, i + 1) for i in range(count - 1)]
        backward = [(target, source) for source, target in forward]
        low = lax.ppermute(
            lax.slice_in_dim(block, block.shape[dim] - width, None, axis=dim), axis, forward
        )
        high = lax.ppermute(lax.slice_in_dim(block, 0, width, axis=dim), axis, backward)
        block = jnp.concatenate([low, block, high], axis=dim)
    return block


def lookup(land_class, conductance):
    cond = jnp.zeros(land_class.shape, jnp.float32)
    for klass in range(CLASSES):
        cond = cond + jnp.where(land_class == klass, conductance[klass], jnp.float32(0.0))
    return cond


def smooth_from(padded, factors, cond):
    rank = factors.shape[1]
    beside_all = padded[:-2] + padded[2:]
    sideways = jnp.pad(padded[1:-1], ((0, 0), (0, 0), (1, 1)))
    beside_all = beside_all + sideways[:, :, :-2] + sideways[:, :, 2:]
    return cond[:, None, :] * (
        beside_all[:, rank : rank + 1, :] * factors - beside_all[:, :rank, :]
    )


def on_device(
    observed, weights, pixel_factors, pixel_bias, date_factors, date_bias, land_class, conductance
):
    rows, rank, cols = pixel_factors.shape
    hi = lax.Precision.HIGHEST
    cond = lookup(land_class, conductance)
    stacked = jnp.concatenate([cond[:, None, :] * pixel_factors, cond[:, None, :]], axis=1)
    padded = extended(stacked, (("space", 0),), 1)
    smooth = smooth_from(padded, pixel_factors, cond)
    pred = jnp.einsum("yrw,rt->ywt", pixel_factors, date_factors, precision=hi)
    pred = pred + pixel_bias[:, :, None] + date_bias
    local_count = jnp.sum(weights, dtype=jnp.float32)
    misfit = weights.astype(jnp.float32) * (pred - observed.astype(jnp.float32))
    pixels = jnp.float32(lax.axis_size("space") * rows * cols)
    count = lax.psum(local_count, "space")
    resid = pixels / count * misfit
    part_fac = jnp.einsum("ywt,yrw->rt", resid, pixel_factors, precision=hi)
    part_bias = jnp.sum(resid, axis=(0, 1))
    grad_date_factors, grad_date_bias = lax.psum((part_fac, part_bias), "space")
    grad_pixel_bias = jnp.sum(resid, axis=2)
    grad_pixel_factors = jnp.einsum("ywt,rt->yrw", resid, date_factors, precision=hi) + smooth
    return (grad_pixel_factors, grad_pixel_bias, grad_date_factors, grad_date_bias)


def solution(mesh):
    return jax.shard_map(
        on_device,
        mesh=mesh,
        in_specs=(
            P(("parts", "space"), None, None),
            P(("parts", "space"), None, None),
            P(("parts", "space"), None, None),
            P(("parts", "space"), None),
            P("parts", None),
            P("parts"),
            P(("parts", "space"), None),
            P(),
        ),
        out_specs=(
            P(("parts", "space"), None, None),
            P(("parts", "space"), None),
            P("parts", None),
            P("parts"),
        ),
        check_vma=False,
    )
```

profile of v0, /device:TPU:0, one launch (start us, length us, event | category | flops | bytes accessed | tf_op | source)
XLA Modules:
  0.0 121.0 jit_solution(1055922444799629655)
XLA Ops:
  0.6 0.0 copy-start
  0.6 1.4 %fusion.11 = (f32[1]{0:T(128)}, f32[1]{0:T(128)}, f32[1]{0:T(128)}, f32[1]{0:T(128)}) fusion(f32[4]{0:T(128)} %param.15), kind=kLoop, calls=%fused_computation.28 | loop fusion | bytes 32 | tf_op jit(solution)/shard_map/slice | solution.py:25
  2.0 3.5 %select_add_fusion = f32[4,4096]{1,0:T(4,128)S(1)} fusion(s32[4,4096]{1,0:T(4,128)} %param.14, f32[]{:T(128)} %bitcast.5, f32[]{:T(128)} %bitcast.4, f32[]{:T(128)} %bitcast.3, f32[]{:T(128)} %bitcast.2), kind=kLoop, calls=%fused_computation.24 | loop fusion | flops 180224 | bytes 131088 | tf_op jit(solution)/shard_map/add | solution.py:25
  5.5 0.0 copy-start.3
  5.6 1.5 %broadcast_multiply_fusion = f32[4,16,4096]{2,1,0:T(8,128)S(1)} fusion(f32[4,16,4096]{2,1,0:T(8,128)} %param.10, f32[4,4096]{1,0:T(4,128)S(1)} %select_add_fusion), kind=kLoop, calls=%fused_computation.20 | loop fusion | flops 262144 | bytes 2162688 | tf_op jit(solution)/shard_map/mul | solution.py:45
  7.1 0.8 fusion.6
  7.9 0.0 copy-start.2
  7.9 0.0 copy-start.4
  7.9 0.0 copy-start.5
  7.9 2.5 %collective-permute-start = (f32[1,17,4096]{2,1,0:T(8,128)}, f32[1,17,4096]{2,1,0:T(8,128)S(1)}, u32[]{:S(2)}, u32[]{:S(2)}) collective-permute-start(f32[1,17,4096]{2,1,0:T(8,128)} %get-tuple-element.8), channel_id=1, source_target_pairs={{0,1},{1,2},{2,3},{3,4},{4,5},{5,6},{6,7},{7,8},{8,9},{9,10},{10,1... | collective-permute-start | bytes 835592 | tf_op jit(solution)/shard_map/ppermute | solution.py:14
  10.4 0.0 copy-done.3
  10.4 2.8 %convert_reduce_fusion = f32[]{:T(128)} fusion(bf16[4,4096,128]{2,1,0:T(8,128)(2,1)S(1)} %copy-done.3), kind=kLoop, calls=%fused_computation.1 | loop fusion | flops 4194303 | bytes 4194308 | tf_op jit(solution)/shard_map/reduce_sum | solution.py:50
  13.2 1.3 %collective-permute-start.1 = (f32[1,17,4096]{2,1,0:T(8,128)S(1)}, f32[1,17,4096]{2,1,0:T(8,128)S(1)}, u32[]{:S(2)}, u32[]{:S(2)}) collective-permute-start(f32[1,17,4096]{2,1,0:T(8,128)S(1)} %get-tuple-element.9), channel_id=1, source_target_pairs={{1,0},{2,1},{3,2},{4,3},{5,4},{6,5},{7,6},{8,7},{9,8},{10,9},{11,1... | collective-permute-start | bytes 835592 | tf_op jit(solution)/shard_map/ppermute | solution.py:17
  14.4 36.4 %psum.21 = f32[]{:T(128)} all-reduce(f32[]{:T(128)} %convert_reduce_fusion), channel_id=1, replica_groups=mesh['parts'=2,'space'=16] {'space'}, use_global_device_ids=true, to_apply=%region_1.2 | all-reduce | flops 1 | bytes 8 | tf_op jit(solution)/shard_map/psum | solution.py:53
  51.6 0.0 copy-done
  51.6 0.0 copy-done.2
  51.6 0.0 copy-done.4
  51.6 0.0 copy-done.5
  51.6 21.1 %fusion.10 = (f32[128]{0:T(128)S(1)}, f32[4,4096]{1,0:T(4,128)}, f32[4,4096,128]{2,1,0:T(8,128)S(1)}) fusion(bf16[4,4096,128]{2,1,0:T(8,128)(2,1)} %param.8, f32[128]{0:T(128)S(1)} %copy-done.5, f32[4,4096]{1,0:T(4,128)S(1)} %copy-done.4, f32[4,16,4096]{2,1,0:T(8,128)S(1)} %copy-done.2, f32[16,128]{1,0:T(8,128)S(1)} %copy-done, ...), kind=kOutput, calls=%fused_computation.27 | convolution fusion | flops 421511040 | bytes 17966084 | tf_op jit(solution)/shard_map/yrw,rt->ywt/dot_general | solution.py:48
  72.7 0.0 copy-start.1
  72.7 4.7 %convolution_bitcast_fusion.1 = f32[16,128]{1,0:T(8,128)S(1)} fusion(f32[4,4096,128]{2,1,0:T(8,128)S(1)} %get-tuple-element.14, f32[4,16,4096]{2,1,0:T(8,128)S(1)} %copy-done.2), kind=kOutput, calls=%fused_computation.17 | convolution fusion | flops 402653184 | bytes 9445376 | tf_op jit(solution)/shard_map/ywt,yrw->rt/dot_general | solution.py:55
  77.4 0.0 copy-done.1
  77.4 31.0 %all-reduce.1 = (f32[16,128]{1,0:T(8,128)}, f32[128]{0:T(128)}) all-reduce(f32[16,128]{1,0:T(8,128)S(1)} %convolution_bitcast_fusion.1, f32[128]{0:T(128)S(1)} %get-tuple-element.4), channel_id=1, replica_groups=mesh['parts'=2,'space'=16] {'space'}, use_global_device_ids=true, to_apply=%region_3.4 | all-reduce | flops 2176 | bytes 17408 | tf_op jit(solution)/shard_map/psum | solution.py:57
  108.4 0.1 pad_maximum_fusion
  108.6 0.0 collective-permute-done
  108.6 0.0 collective-permute-done.1
  108.6 0.9 fusion.4
  109.6 11.5 %fusion.1 = f32[4,16,4096]{2,1,0:T(8,128)} fusion(f32[4,4096,128]{2,1,0:T(8,128)} %copy-done.1, f32[4,17,4096]{2,1,0:T(8,128)S(1)} %fusion.4, f32[4,16,4096]{2,1,0:T(8,128)S(1)} %copy-done.2, f32[4,4096]{1,0:T(4,128)S(1)} %bitcast.26, f32[4,4096]{1,0:T(4,128)S(1)} %select_add_fusion, f32[16,128]{1,0:T(8,128)S(1)} %copy-done), kind=kOutput, calls=%fused_computation.4 | convolution fusion | flops 403701760 | bytes 11673600 | tf_op jit(solution)/shard_map/ywt,rt->yrw/dot_general | solution.py:59
  (3 shorter events, 0.1 us)
Async XLA Ops:
  0.6 50.9 %copy-start = (f32[16,128]{1,0:T(8,128)S(1)}, f32[16,128]{1,0:T(8,128)}, u32[]{:S(2)}) copy-start(f32[16,128]{1,0:T(8,128)} %param.12) | copy-start | bytes 24580
  5.5 4.9 %copy-start.3 = (bf16[4,4096,128]{2,1,0:T(8,128)(2,1)S(1)}, bf16[4,4096,128]{2,1,0:T(8,128)(2,1)}, u32[]{:S(2)}) copy-start(bf16[4,4096,128]{2,1,0:T(8,128)(2,1)} %param.9) | copy-start | bytes 12582916
  7.9 43.7 %copy-start.2 = (f32[4,16,4096]{2,1,0:T(8,128)S(1)}, f32[4,16,4096]{2,1,0:T(8,128)}, u32[]{:S(2)}) copy-start(f32[4,16,4096]{2,1,0:T(8,128)} %param.10) | copy-start | bytes 3145732
  7.9 43.7 %copy-start.4 = (f32[4,4096]{1,0:T(4,128)S(1)}, f32[4,4096]{1,0:T(4,128)}, u32[]{:S(2)}) copy-start(f32[4,4096]{1,0:T(4,128)} %param.11) | copy-start | bytes 196612
  7.9 43.7 %copy-start.5 = (f32[128]{0:T(128)S(1)}, f32[128]{0:T(128)}, u32[]{:S(2)}) copy-start(f32[128]{0:T(128)} %param.13) | copy-start | bytes 1540
  7.9 100.7 %collective-permute-start = (f32[1,17,4096]{2,1,0:T(8,128)}, f32[1,17,4096]{2,1,0:T(8,128)S(1)}, u32[]{:S(2)}, u32[]{:S(2)}) collective-permute-start(f32[1,17,4096]{2,1,0:T(8,128)} %get-tuple-element.8), channel_id=1, source_target_pairs={{0,1},{1,2},{2,3},{3,4},{4,5},{5,6},{6,7},{7,8},{8,9},{9,10},{10,1... | collective-permute-start | bytes 835592 | tf_op jit(solution)/shard_map/ppermute | solution.py:14
  13.2 95.4 %collective-permute-start.1 = (f32[1,17,4096]{2,1,0:T(8,128)S(1)}, f32[1,17,4096]{2,1,0:T(8,128)S(1)}, u32[]{:S(2)}, u32[]{:S(2)}) collective-permute-start(f32[1,17,4096]{2,1,0:T(8,128)S(1)} %get-tuple-element.9), channel_id=1, source_target_pairs={{1,0},{2,1},{3,2},{4,3},{5,4},{6,5},{7,6},{8,7},{9,8},{10,9},{11,1... | collective-permute-start | bytes 835592 | tf_op jit(solution)/shard_map/ppermute | solution.py:17
  72.7 4.7 %copy-start.1 = (f32[4,4096,128]{2,1,0:T(8,128)}, f32[4,4096,128]{2,1,0:T(8,128)S(1)}, u32[]{:S(2)}) copy-start(f32[4,4096,128]{2,1,0:T(8,128)S(1)} %get-tuple-element.14) | copy-start | bytes 25165828
where the time goes:
time: 121 us
  blocking collectives  67.5 us (56%)
  matrix products  37.2 us (31%)
  other arithmetic  9.54 us (8%)
  starting transfers between devices  3.78 us (3%)
  local copies, waits for them, and re-layouts  1.55 us (1%)
  between operations  1.47 us (1%)
    psum x1, blocking collectives, on_device(): count = lax.psum(local_count, 'space')  36.4 us
    psum x1, blocking collectives, on_device(): grad_date_factors, grad_date_bias = lax.psum((part_fac, part_bias), 'space')  31 us
    dot_general x1, matrix products, on_device(): pred = jnp.einsum('yrw,rt->ywt', pixel_factors, date_factors, precision=hi)  21.1 us
    dot_general x1, matrix products, on_device(): jnp.einsum('ywt,rt->yrw', resid, date_factors, precision=hi) + smooth  11.5 us
    dot_general x1, matrix products, on_device(): part_fac = jnp.einsum('ywt,yrw->rt', resid, pixel_factors, precision=hi)  4.7 us
    add x1, other arithmetic, lookup(): cond + jnp.where(land_class == klass, conductance[klass], jnp.float32(0.0))  3.48 us
    reduce_sum x1, other arithmetic, on_device(): local_count = jnp.sum(weights, dtype=jnp.float32)  2.75 us
    ppermute x1, starting transfers between devices, extended(): lax.ppermute(lax.slice_in_dim(block, block.shape[dim] - width, None, axis...  2.5 us
  transfers between devices with their start and end apart: 2, of which 0 were waited for; matrix products, arithmetic and copies ran while one was open for 24% of the time, Pallas kernels for 0%

commit v1 on v0

v1 whole, which is shorter than its diff:
```python
import functools

import jax
import jax.numpy as jnp
from jax import lax
from jax.experimental import pallas as pl
from jax.experimental.pallas import tpu as pltpu
from jax.sharding import PartitionSpec as P

CLASSES = 4
CHUNK = 1024
MIB = 1024 * 1024


def split(x):
    head = x.astype(jnp.bfloat16)
    return head, (x - head.astype(jnp.float32)).astype(jnp.bfloat16)


def lookup(land_class, cond_ref):
    cond = jnp.zeros(land_class.shape, jnp.float32)
    for klass in range(CLASSES):
        cond = cond + jnp.where(land_class == klass, cond_ref[klass], jnp.float32(0.0))
    return cond


def beside(x):
    cols = x.shape[1]
    col = lax.broadcasted_iota(jnp.int32, x.shape, 1)
    left = jnp.where(col == 0, 0.0, pltpu.roll(x, 1, 1))
    right = jnp.where(col == cols - 1, 0.0, pltpu.roll(x, cols - 1, 1))
    return left + right


def kernel(
    n, group, chunk,
    cond_ref, obs_hbm, wts_hbm, fac_hbm, pb_hbm, df_ref, db_ref, lc_hbm,
    u_hbm, s_hbm, g_ref, gdf_ref, gdb_ref, scale_ref,
    obs, wts, fac, pb, lc, unscaled, smooth, halo_f, halo_c, rhs, back, stage_a, stage_b, cond,
    obs_sem, wts_sem, fac_sem, small_sem, u_sem, s_sem,
    halo_send, halo_recv, a_send, a_recv, b_send, b_recv,
):
    rows, rank, cols = fac.shape
    dates = obs.shape[2]
    per_row = cols // chunk
    steps = rows * per_row
    half = chunk // 2
    groups = n // group
    f32, bf16 = jnp.float32, jnp.bfloat16

    me = lax.axis_index("space")
    above = lax.rem(me + n - 1, n)
    below = lax.rem(me + 1, n)
    mine_a = lax.rem(me, group)
    mine_b = me // group
    peers_a = [mine_b * group + lax.rem(mine_a + k, group) for k in range(1, group)]
    peers_b = [lax.rem(mine_b + k, groups) * group + mine_a for k in range(1, groups)]

    barrier = pltpu.get_barrier_semaphore()
    greeted = [above, below] + peers_a + peers_b
    for peer in greeted:
        pl.semaphore_signal(
            barrier, inc=1, device_id={"space": peer}, device_id_type=pl.DeviceIdType.MESH
        )

    def chunk_copies(y, c, step):
        at = pl.ds(pl.multiple_of(c * chunk, chunk), chunk)
        return (
            pltpu.make_async_copy(obs_hbm.at[y, at], obs.at[y, at], obs_sem.at[step]),
            pltpu.make_async_copy(wts_hbm.at[y, at], wts.at[y, at], wts_sem.at[step]),
        )

    pb_copy = pltpu.make_async_copy(pb_hbm, pb, small_sem.at[0])
    lc_copy = pltpu.make_async_copy(lc_hbm, lc, small_sem.at[1])
    fac_copies = [
        pltpu.make_async_copy(fac_hbm.at[y], fac.at[y], fac_sem.at[y]) for y in range(rows)
    ]
    pb_copy.start()
    fac_copies[0].start()
    for y in range(rows):
        for c in range(per_row):
            for copy in chunk_copies(y, c, y * per_row + c):
                copy.start()
        if y + 1 < rows:
            fac_copies[y + 1].start()
    lc_copy.start()

    dh, dl = split(df_ref[...])
    bh, bl = split(db_ref[...])
    line = lax.broadcasted_iota(jnp.int32, (16, dates), 0)
    tail = jnp.where(
        line < 2, 1.0,
        jnp.where(line == 2, bh.astype(f32), jnp.where(line == 3, bl.astype(f32), 0.0)),
    ).astype(bf16)
    one = jnp.concatenate([dh, dh, dl, tail], axis=0)
    none = jnp.zeros_like(one)
    rhs[...] = jnp.concatenate(
        [jnp.concatenate([one, none], axis=1), jnp.concatenate([none, one], axis=1)], axis=0
    )
    ones_line = jnp.where(line == 0, 1.0, 0.0).astype(bf16)
    back[...] = jnp.concatenate(
        [
            jnp.concatenate([dh, dh], axis=1),
            jnp.concatenate([dl, jnp.zeros_like(dl)], axis=1),
            jnp.concatenate([ones_line, ones_line], axis=1),
        ],
        axis=0,
    )

    pl.semaphore_wait(barrier, len(greeted))

    def remote(src, dst, send, recv, peer):
        return pltpu.make_async_remote_copy(
            src_ref=src, dst_ref=dst, send_sem=send, recv_sem=recv,
            device_id={"space": peer}, device_id_type=pl.DeviceIdType.MESH,
        )

    halo = [
        remote(fac_hbm.at[0], halo_f.at[1], halo_send.at[0], halo_recv.at[0], above),
        remote(fac_hbm.at[rows - 1], halo_f.at[0], halo_send.at[1], halo_recv.at[1], below),
        remote(lc_hbm, halo_c.at[1], halo_send.at[2], halo_recv.at[2], above),
        remote(lc_hbm, halo_c.at[0], halo_send.at[3], halo_recv.at[3], below),
    ]
    for copy in halo:
        copy.start()
    pb_copy.wait()

    slot = lax.broadcasted_iota(jnp.int32, (16, chunk), 0)

    def u_copy(y, c, step):
        at = pl.ds(pl.multiple_of(c * chunk, chunk), chunk)
        return pltpu.make_async_copy(unscaled.at[y, :, at], u_hbm.at[y, :, at], u_sem.at[step])

    def body(y, c, carry):
        total, count = carry
        step = y * per_row + c
        for copy in chunk_copies(y, c, step):
            copy.wait()
        start = pl.multiple_of(c * chunk, chunk)
        fh, fl = split(fac[y, :, pl.ds(start, chunk)])
        ph, plow = split(pb[pl.ds(y, 1), pl.ds(start, chunk)])
        extra = jnp.where(
            slot == 0, ph.astype(f32),
            jnp.where(slot == 1, plow.astype(f32), jnp.where(slot < 4, 1.0, 0.0)),
        ).astype(bf16)
        lhs = jnp.concatenate([fh, fl, fh, extra], axis=0)
        halves = [lhs[:, :half], lhs[:, half:]]
        pred = lax.dot_general(
            jnp.concatenate(halves, axis=0), rhs[...], (((0,), (0,)), ((), ())),
            preferred_element_type=f32,
        )
        for j in range(2):
            at = pl.ds(pl.multiple_of(start + j * half, half), half)
            w = wts[y, at, :].astype(f32)
            count = count + jnp.sum(w.reshape(half // 8, 8, dates), axis=0)
            misfit = w * (pred[:, j * dates : (j + 1) * dates] - obs[y, at, :].astype(f32))
            mh, ml = split(misfit)
            both = jnp.concatenate([mh, ml], axis=1)
            total = total + lax.dot_general(
                halves[j], both, (((1,), (0,)), ((), ())), preferred_element_type=f32
            )
            pix = lax.dot_general(
                back[...], both, (((1,), (1,)), ((), ())), preferred_element_type=f32
            )
            unscaled[y, :, at] = pix[:rank] + pix[rank : 2 * rank]
            g_ref[pl.ds(y, 1), at] = pix[2 * rank : 2 * rank + 1]
        u_copy(y, c, step).start()
        return total, count

    carry = (jnp.zeros((64, 2 * dates), f32), jnp.zeros((8, dates), f32))
    for y in range(rows):
        fac_copies[y].wait()
        carry = lax.fori_loop(0, per_row, functools.partial(body, y), carry)
    total, count = carry

    gdf = total[:rank, :dates] + total[:rank, dates:] + total[rank : 2 * rank, :dates]
    gdb = total[50:51, :dates] + total[50:51, dates:]
    line8 = lax.broadcasted_iota(jnp.int32, (8, dates), 0)
    last = jnp.where(
        line8 == 0, gdb, jnp.where(line8 == 1, jnp.sum(count, axis=0, keepdims=True), 0.0)
    )
    stage_a[mine_a] = jnp.concatenate([gdf, last], axis=0)
    sends_a = [
        remote(stage_a.at[mine_a], stage_a.at[mine_a], a_send.at[k], a_recv.at[k], peer)
        for k, peer in enumerate(peers_a)
    ]
    for copy in sends_a:
        copy.start()

    lc_copy.wait()
    for copy in halo:
        copy.wait()
    cond[0:1] = jnp.where(me == 0, 0.0, lookup(halo_c[0, rows - 1 : rows, :], cond_ref))
    cond[rows + 1 : rows + 2] = jnp.where(me == n - 1, 0.0, lookup(halo_c[1, 0:1, :], cond_ref))
    cond[1 : rows + 1] = lookup(lc[...], cond_ref)

    def row_factors(y):
        return halo_f[0] if y < 0 else halo_f[1] if y == rows else fac[y]

    def smooth_row(y):
        own = cond[y + 1 : y + 2]
        north, south = cond[y : y + 1], cond[y + 2 : y + 3]
        f = fac[y]
        around = north + south + beside(own)
        weighted = north * row_factors(y - 1) + south * row_factors(y + 1) + beside(own * f)
        smooth[y] = own * (around * f - weighted)
        copy = pltpu.make_async_copy(smooth.at[y], s_hbm.at[y], s_sem.at[y])
        copy.start()
        return copy

    s_copies = [smooth_row(y) for y in range(rows // 2)]

    for copy in sends_a:
        copy.wait()
    part = stage_a[0]
    for k in range(1, group):
        part = part + stage_a[k]
    stage_b[mine_b] = part
    sends_b = [
        remote(stage_b.at[mine_b], stage_b.at[mine_b], b_send.at[k], b_recv.at[k], peer)
        for k, peer in enumerate(peers_b)
    ]
    for copy in sends_b:
        copy.start()

    s_copies += [smooth_row(y) for y in range(rows // 2, rows)]

    for copy in sends_b:
        copy.wait()
    part = stage_b[0]
    for k in range(1, groups):
        part = part + stage_b[k]
    clear = jnp.sum(part[rank + 1 : rank + 2], axis=1, keepdims=True)
    scale = jnp.float32(n * rows * cols) / clear
    gdf_ref[...] = scale * part[:rank]
    gdb_ref[...] = scale * part[rank : rank + 1]
    scale_ref[...] = jnp.broadcast_to(scale, scale_ref.shape)

    for y in range(rows):
        for c in range(per_row):
            u_copy(y, c, y * per_row + c).wait()
    for copy in s_copies:
        copy.wait()


def on_device(
    observed, weights, pixel_factors, pixel_bias, date_factors, date_bias, land_class, conductance
):
    rows, rank, cols = pixel_factors.shape
    dates = observed.shape[2]
    n = lax.axis_size("space")
    group = max(d for d in range(1, n + 1) if n % d == 0 and d * d <= n)
    groups = n // group
    chunk = min(CHUNK, cols)
    steps = rows * (cols // chunk)
    f32, bf16 = jnp.float32, jnp.bfloat16
    dma = pltpu.SemaphoreType.DMA
    hbm = pl.BlockSpec(memory_space=pl.ANY)
    vmem = pl.BlockSpec(memory_space=pltpu.VMEM)
    u, s, g, gdf, gdb, scale = pl.pallas_call(
        functools.partial(kernel, n, group, chunk),
        out_shape=(
            jax.ShapeDtypeStruct((rows, rank, cols), f32),
            jax.ShapeDtypeStruct((rows, rank, cols), f32),
            jax.ShapeDtypeStruct((rows, cols), f32),
            jax.ShapeDtypeStruct((rank, dates), f32),
            jax.ShapeDtypeStruct((1, dates), f32),
            jax.ShapeDtypeStruct((8, 128), f32),
        ),
        in_specs=[
            pl.BlockSpec(memory_space=pltpu.SMEM), hbm, hbm, hbm, hbm, vmem, vmem, hbm,
        ],
        out_specs=(hbm, hbm, vmem, vmem, vmem, vmem),
        scratch_shapes=[
            pltpu.VMEM((rows, cols, dates), bf16),
            pltpu.VMEM((rows, cols, dates), bf16),
            pltpu.VMEM((rows, rank, cols), f32),
            pltpu.VMEM((rows, cols), f32),
            pltpu.VMEM((rows, cols), jnp.int32),
            pltpu.VMEM((rows, rank, cols), f32),
            pltpu.VMEM((rows, rank, cols), f32),
            pltpu.VMEM((2, rank, cols), f32),
            pltpu.VMEM((2, rows, cols), jnp.int32),
            pltpu.VMEM((128, 2 * dates), bf16),
            pltpu.VMEM((48, 2 * dates), bf16),
            pltpu.VMEM((group, 24, dates), f32),
            pltpu.VMEM((groups, 24, dates), f32),
            pltpu.VMEM((rows + 2, cols), f32),
            dma((steps,)), dma((steps,)), dma((rows,)), dma((2,)), dma((steps,)), dma((rows,)),
            dma((4,)), dma((4,)),
            dma((group,)), dma((group,)), dma((groups,)), dma((groups,)),
        ],
        compiler_params=pltpu.CompilerParams(
            collective_id=0, has_side_effects=True, vmem_limit_bytes=40 * MIB
        ),
        name="gap_fill",
    )(
        conductance, observed, weights, pixel_factors, pixel_bias, date_factors,
        date_bias.reshape(1, dates), land_class,
    )
    scale = scale[0, 0]
    return scale * u + s, scale * g, gdf, gdb.reshape(dates)


def solution(mesh):
    return jax.shard_map(
        on_device,
        mesh=mesh,
        in_specs=(
            P(("parts", "space"), None, None),
            P(("parts", "space"), None, None),
            P(("parts", "space"), None, None),
            P(("parts", "space"), None),
            P("parts", None),
            P("parts"),
            P(("parts", "space"), None),
            P(),
        ),
        out_specs=(
            P(("parts", "space"), None, None),
            P(("parts", "space"), None),
            P("parts", None),
            P("parts"),
        ),
        check_vma=False,
    )
```

time: 121 us -> 38.2 us (0.32)
  blocking collectives: 67.5 us -> 0 us
  matrix products: 37.2 us -> 0 us
  Pallas kernels: 0 us -> 23.3 us
  local copies, waits for them, and re-layouts: 1.55 us -> 10.9 us
  other arithmetic: 9.54 us -> 3.01 us
  starting transfers between devices: 3.78 us -> 0 us
    psum x2 -> x0, blocking collectives: 67.5 us -> none  [the longest x1 36.4 us: on_device(): count = lax.psum(local_count, 'space')]
    dot_general x3 -> x0, matrix products: 37.2 us -> none  [the longest x1 21.1 us: on_device(): pred = jnp.einsum('yrw,rt->ywt', pixel_factors, date_factors, precision=hi)]
    pallas_call x0 -> x1, Pallas kernels: none -> 23.3 us  [on_device(): pl.pallas_call(functools.partial(kernel, n, group, chunk), out_shape=(jax...]
    unnamed x13 -> x18, local copies, waits for them, and re-layouts: 0.08 us -> 10.4 us
    ppermute x2 -> x0, starting transfers between devices: 3.78 us -> none  [the longest x1 2.5 us: extended(): lax.ppermute(lax.slice_in_dim(block, block.shape[dim] - width, None, axis...]
    reduce_sum x1 -> x0, other arithmetic: 2.75 us -> none  [on_device(): local_count = jnp.sum(weights, dtype=jnp.float32)]
    add x2 -> x1, other arithmetic: 4.36 us -> 1.72 us  [on_device(): return (scale * u + s, scale * g, gdf, gdb.reshape(dates))]
  transfers between devices with their start and end apart: 2 -> 0, of which waited for: 0 -> 0; matrix products, arithmetic and copies ran while one was open for 24% -> 0% of each run, Pallas kernels for 0% -> 0%
where the time goes in v1:
time: 38.2 us; the launch traced here: 37.8 us
  Pallas kernels  23.3 us (61%)
  local copies, waits for them, and re-layouts  10.9 us (29%)
  other arithmetic  3.01 us (8%)
  between operations  0.66 us (2%)
    pallas_call x1, Pallas kernels, on_device(): pl.pallas_call(functools.partial(kernel, n, group, chunk), out_shape=(jax...  23.3 us
    unnamed x18, local copies, waits for them, and re-layouts  10.4 us
    add x1, other arithmetic, on_device(): return (scale * u + s, scale * g, gdf, gdb.reshape(dates))  1.72 us
    mul x1, other arithmetic, on_device(): return (scale * u + s, scale * g, gdf, gdb.reshape(dates))  1.29 us

profile of v1, /device:TPU:0, one launch (start us, length us, event | category | flops | bytes accessed | tf_op | source)
XLA Modules:
  0.0 37.8 jit_solution(15888449420902302699)
XLA Ops:
  0.6 0.0 copy-start
  0.6 2.2 %copy-done = bf16[4,4096,128]{2,1,0:T(8,128)(2,1)S(1)} copy-done((bf16[4,4096,128]{2,1,0:T(8,128)(2,1)S(1)}, bf16[4,4096,128]{2,1,0:T(8,128)(2,1)}, u32[]{:S(2)}) %copy-start) | copy-done | bytes 4194328
  2.8 0.0 copy-start.1
  2.8 2.2 %copy-done.1 = bf16[4,4096,128]{2,1,0:T(8,128)(2,1)S(1)} copy-done((bf16[4,4096,128]{2,1,0:T(8,128)(2,1)S(1)}, bf16[4,4096,128]{2,1,0:T(8,128)(2,1)}, u32[]{:S(2)}) %copy-start.1) | copy-done | bytes 4194328
  5.0 0.0 copy-start.2
  5.0 1.2 %copy-done.2 = f32[4,16,4096]{2,1,0:T(8,128)S(1)} copy-done((f32[4,16,4096]{2,1,0:T(8,128)S(1)}, f32[4,16,4096]{2,1,0:T(8,128)}, u32[]{:S(2)}) %copy-start.2) | copy-done | bytes 1048600
  6.2 0.0 copy-start.3
  6.2 0.8 %copy-done.3 = f32[4,4096]{1,0:T(4,128)S(1)} copy-done((f32[4,4096]{1,0:T(4,128)S(1)}, f32[4,4096]{1,0:T(4,128)}, u32[]{:S(2)}) %copy-start.3) | copy-done | bytes 65560
  7.1 0.0 copy-start.4
  7.1 0.8 %copy-done.4 = s32[4,4096]{1,0:T(4,128)S(1)} copy-done((s32[4,4096]{1,0:T(4,128)S(1)}, s32[4,4096]{1,0:T(4,128)}, u32[]{:S(2)}) %copy-start.4) | copy-done | bytes 65560
  7.9 0.0 copy-start.5
  7.9 0.7 %copy-done.5 = f32[16,128]{1,0:T(8,128)S(1)} copy-done((f32[16,128]{1,0:T(8,128)S(1)}, f32[16,128]{1,0:T(8,128)}, u32[]{:S(2)}) %copy-start.5) | copy-done | bytes 8216
  8.6 0.0 copy-start.6
  8.6 0.7 %copy-done.6 = f32[4]{0:T(128)S(1)} copy-done((f32[4]{0:T(128)S(1)}, f32[4]{0:T(128)}, u32[]{:S(2)}) %copy-start.6) | copy-done | bytes 40
  9.3 0.0 copy-start.7
  9.3 0.7 %copy-done.7 = f32[128]{0:T(128)S(1)} copy-done((f32[128]{0:T(128)S(1)}, f32[128]{0:T(128)}, u32[]{:S(2)}) %copy-start.7) | copy-done | bytes 536
  9.9 23.3 %gap_fill.1 = (f32[4,16,4096]{2,1,0:T(8,128)S(1)}, f32[4,16,4096]{2,1,0:T(8,128)S(1)}, f32[4,4096]{1,0:T(4,128)S(1)}, f32[16,128]{1,0:T(8,128)S(1)}, f32[1,128]{1,0:T(1,128)S(1)}, /*index=5*/f32[8,128]{1,0:T(8,128)S(1)}) custom-call(f32[4]{0:T(128)S(1)} %copy-done.6, bf16[4,4096,128]{2,1,0:T(8,128)(2,1)S(1)} %copy-done, bf16[4,4096,128]{2,1,0:T(8,128)(2,1)S(1)} %copy-done.1, ...), custom_call_target="tpu_custom_call" | custom-call | tf_op jit(solution)/shard_map/gap_fill/pallas_call | solution.py:260
  33.2 0.5 %slice.3 = f32[1,1]{1,0:T(1,128)} slice(f32[8,128]{1,0:T(8,128)S(1)} %get-tuple-element.10), slice={[0:1], [0:1]} | slice | bytes 8 | tf_op jit(solution)/shard_map/slice | solution.py:301
  33.7 1.7 %multiply_add_fusion = f32[4,16,4096]{2,1,0:T(8,128)} fusion(f32[4,16,4096]{2,1,0:T(8,128)S(1)} %get-tuple-element.12, f32[4,16,4096]{2,1,0:T(8,128)S(1)} %get-tuple-element.11, f32[]{:T(128)} %bitcast.1), kind=kLoop, calls=%fused_computation | loop fusion | flops 524288 | bytes 3145732 | tf_op jit(solution)/shard_map/add | solution.py:302
  35.4 1.3 %broadcast_multiply_fusion = f32[4,4096]{1,0:T(4,128)} fusion(f32[4,4096]{1,0:T(4,128)S(1)} %get-tuple-element.13, f32[]{:T(128)} %bitcast.1), kind=kLoop, calls=%fused_computation.1 | loop fusion | flops 16384 | bytes 131076 | tf_op jit(solution)/shard_map/mul | solution.py:302
  36.7 0.6 %copy.14 = f32[16,128]{1,0:T(8,128)} copy(f32[16,128]{1,0:T(8,128)S(1)} %get-tuple-element.22) | data formatting | bytes 16384
  37.3 0.5 %copy.15 = f32[128]{0:T(128)} copy(f32[128]{0:T(128)S(1)} %bitcast.4) | data formatting | bytes 1024
Async XLA Ops:
  0.6 2.2 %copy-start = (bf16[4,4096,128]{2,1,0:T(8,128)(2,1)S(1)}, bf16[4,4096,128]{2,1,0:T(8,128)(2,1)}, u32[]{:S(2)}) copy-start(bf16[4,4096,128]{2,1,0:T(8,128)(2,1)} %obs_hbm.1) | copy-start | bytes 12582916
  2.8 2.2 %copy-start.1 = (bf16[4,4096,128]{2,1,0:T(8,128)(2,1)S(1)}, bf16[4,4096,128]{2,1,0:T(8,128)(2,1)}, u32[]{:S(2)}) copy-start(bf16[4,4096,128]{2,1,0:T(8,128)(2,1)} %wts_hbm.1) | copy-start | bytes 12582916
  5.0 1.2 %copy-start.2 = (f32[4,16,4096]{2,1,0:T(8,128)S(1)}, f32[4,16,4096]{2,1,0:T(8,128)}, u32[]{:S(2)}) copy-start(f32[4,16,4096]{2,1,0:T(8,128)} %fac_hbm.1) | copy-start | bytes 3145732
  6.2 0.8 %copy-start.3 = (f32[4,4096]{1,0:T(4,128)S(1)}, f32[4,4096]{1,0:T(4,128)}, u32[]{:S(2)}) copy-start(f32[4,4096]{1,0:T(4,128)} %pb_hbm.1) | copy-start | bytes 196612
  7.1 0.8 %copy-start.4 = (s32[4,4096]{1,0:T(4,128)S(1)}, s32[4,4096]{1,0:T(4,128)}, u32[]{:S(2)}) copy-start(s32[4,4096]{1,0:T(4,128)} %lc_hbm.1) | copy-start | bytes 196612
  7.9 0.7 %copy-start.5 = (f32[16,128]{1,0:T(8,128)S(1)}, f32[16,128]{1,0:T(8,128)}, u32[]{:S(2)}) copy-start(f32[16,128]{1,0:T(8,128)} %df_ref.1) | copy-start | bytes 24580
  8.6 0.7 %copy-start.6 = (f32[4]{0:T(128)S(1)}, f32[4]{0:T(128)}, u32[]{:S(2)}) copy-start(f32[4]{0:T(128)} %cond_ref.1) | copy-start | bytes 52
  9.3 0.7 %copy-start.7 = (f32[128]{0:T(128)S(1)}, f32[128]{0:T(128)}, u32[]{:S(2)}) copy-start(f32[128]{0:T(128)} %param.13) | copy-start | bytes 1540

commit v2 on v1

--- a/solution.py
+++ b/solution.py
@@ -9,7 +9,7 @@
 
 CLASSES = 4
 CHUNK = 1024
-MIB = 1024 * 1024
+GRANT = 44 * 1024 * 1024
 
 
 def split(x):
@@ -34,10 +34,11 @@
 
 def kernel(
     n, group, chunk,
-    cond_ref, obs_hbm, wts_hbm, fac_hbm, pb_hbm, df_ref, db_ref, lc_hbm,
-    u_hbm, s_hbm, g_ref, gdf_ref, gdb_ref, scale_ref,
-    obs, wts, fac, pb, lc, unscaled, smooth, halo_f, halo_c, rhs, back, stage_a, stage_b, cond,
-    obs_sem, wts_sem, fac_sem, small_sem, u_sem, s_sem,
+    cond_hbm, obs_hbm, wts_hbm, fac_hbm, pb_hbm, df_hbm, db_hbm, lc_hbm,
+    gpf_ref, gpb_ref, gdf_ref, gdb_ref,
+    cond_ref, df_ref, db_ref,
+    obs, wts, fac, pb, lc, smooth, halo_f, halo_c, rhs, back, stage_a, stage_b, cond,
+    obs_sem, wts_sem, fac_sem, small_sem,
     halo_send, halo_recv, a_send, a_recv, b_send, b_recv,
 ):
     rows, rank, cols = fac.shape
@@ -70,11 +71,16 @@
             pltpu.make_async_copy(wts_hbm.at[y, at], wts.at[y, at], wts_sem.at[step]),
         )
 
+    df_copy = pltpu.make_async_copy(df_hbm, df_ref, small_sem.at[2])
+    db_copy = pltpu.make_async_copy(db_hbm, db_ref, small_sem.at[3])
+    cond_copy = pltpu.make_async_copy(cond_hbm, cond_ref, small_sem.at[4])
     pb_copy = pltpu.make_async_copy(pb_hbm, pb, small_sem.at[0])
     lc_copy = pltpu.make_async_copy(lc_hbm, lc, small_sem.at[1])
     fac_copies = [
         pltpu.make_async_copy(fac_hbm.at[y], fac.at[y], fac_sem.at[y]) for y in range(rows)
     ]
+    df_copy.start()
+    db_copy.start()
     pb_copy.start()
     fac_copies[0].start()
     for y in range(rows):
@@ -84,7 +90,10 @@
         if y + 1 < rows:
             fac_copies[y + 1].start()
     lc_copy.start()
-
+    cond_copy.start()
+
+    df_copy.wait()
+    db_copy.wait()
     dh, dl = split(df_ref[...])
     bh, bl = split(db_ref[...])
     line = lax.broadcasted_iota(jnp.int32, (16, dates), 0)
@@ -126,10 +135,6 @@
     pb_copy.wait()
 
     slot = lax.broadcasted_iota(jnp.int32, (16, chunk), 0)
-
-    def u_copy(y, c, step):
-        at = pl.ds(pl.multiple_of(c * chunk, chunk), chunk)
-        return pltpu.make_async_copy(unscaled.at[y, :, at], u_hbm.at[y, :, at], u_sem.at[step])
 
     def body(y, c, carry):
         total, count = carry
@@ -162,9 +167,8 @@
             pix = lax.dot_general(
                 back[...], both, (((1,), (1,)), ((), ())), preferred_element_type=f32
             )
-            unscaled[y, :, at] = pix[:rank] + pix[rank : 2 * rank]
-            g_ref[pl.ds(y, 1), at] = pix[2 * rank : 2 * rank + 1]
-        u_copy(y, c, step).start()
+            gpf_ref[y, :, at] = pix[:rank] + pix[rank : 2 * rank]
+            gpb_ref[pl.ds(y, 1), at] = pix[2 * rank : 2 * rank + 1]
         return total, count
 
     carry = (jnp.zeros((64, 2 * dates), f32), jnp.zeros((8, dates), f32))
@@ -188,6 +192,7 @@
         copy.start()
 
     lc_copy.wait()
+    cond_copy.wait()
     for copy in halo:
         copy.wait()
     cond[0:1] = jnp.where(me == 0, 0.0, lookup(halo_c[0, rows - 1 : rows, :], cond_ref))
@@ -204,11 +209,9 @@
         around = north + south + beside(own)
         weighted = north * row_factors(y - 1) + south * row_factors(y + 1) + beside(own * f)
         smooth[y] = own * (around * f - weighted)
-        copy = pltpu.make_async_copy(smooth.at[y], s_hbm.at[y], s_sem.at[y])
-        copy.start()
-        return copy
-
-    s_copies = [smooth_row(y) for y in range(rows // 2)]
+
+    for y in range(rows // 2):
+        smooth_row(y)
 
     for copy in sends_a:
         copy.wait()
@@ -223,7 +226,8 @@
     for copy in sends_b:
         copy.start()
 
-    s_copies += [smooth_row(y) for y in range(rows // 2, rows)]
+    for y in range(rows // 2, rows):
+        smooth_row(y)
 
     for copy in sends_b:
         copy.wait()
@@ -234,12 +238,20 @@
     scale = jnp.float32(n * rows * cols) / clear
     gdf_ref[...] = scale * part[:rank]
     gdb_ref[...] = scale * part[rank : rank + 1]
-    scale_ref[...] = jnp.broadcast_to(scale, scale_ref.shape)
-
+    gpb_ref[...] = scale * gpb_ref[...]
     for y in range(rows):
-        for c in range(per_row):
-            u_copy(y, c, y * per_row + c).wait()
-    for copy in s_copies:
+        gpf_ref[y] = scale * gpf_ref[y] + smooth[y]
+
+
+def place(*refs):
+    half = len(refs) // 2
+    sem = refs[-1]
+    copies = [
+        pltpu.make_async_copy(refs[i], refs[half + i], sem.at[i]) for i in range(half)
+    ]
+    for copy in copies:
+        copy.start()
+    for copy in copies:
         copy.wait()
 
 
@@ -255,29 +267,28 @@
     steps = rows * (cols // chunk)
     f32, bf16 = jnp.float32, jnp.bfloat16
     dma = pltpu.SemaphoreType.DMA
-    hbm = pl.BlockSpec(memory_space=pl.ANY)
+    anywhere = pl.BlockSpec(memory_space=pl.ANY)
     vmem = pl.BlockSpec(memory_space=pltpu.VMEM)
-    u, s, g, gdf, gdb, scale = pl.pallas_call(
+    shapes = (
+        jax.ShapeDtypeStruct((rows, rank, cols), f32),
+        jax.ShapeDtypeStruct((rows, cols), f32),
+        jax.ShapeDtypeStruct((rank, dates), f32),
+        jax.ShapeDtypeStruct((1, dates), f32),
+    )
+    grads = pl.pallas_call(
         functools.partial(kernel, n, group, chunk),
-        out_shape=(
-            jax.ShapeDtypeStruct((rows, rank, cols), f32),
-            jax.ShapeDtypeStruct((rows, rank, cols), f32),
-            jax.ShapeDtypeStruct((rows, cols), f32),
-            jax.ShapeDtypeStruct((rank, dates), f32),
-            jax.ShapeDtypeStruct((1, dates), f32),
-            jax.ShapeDtypeStruct((8, 128), f32),
-        ),
-        in_specs=[
-            pl.BlockSpec(memory_space=pltpu.SMEM), hbm, hbm, hbm, hbm, vmem, vmem, hbm,
-        ],
-        out_specs=(hbm, hbm, vmem, vmem, vmem, vmem),
+        out_shape=tuple(pltpu.VMEM(x.shape, x.dtype) for x in shapes),
+        in_specs=[anywhere] * 8,
+        out_specs=(vmem,) * 4,
         scratch_shapes=[
+            pltpu.SMEM((CLASSES,), f32),
+            pltpu.VMEM((rank, dates), f32),
+            pltpu.VMEM((1, dates), f32),
             pltpu.VMEM((rows, cols, dates), bf16),
             pltpu.VMEM((rows, cols, dates), bf16),
             pltpu.VMEM((rows, rank, cols), f32),
             pltpu.VMEM((rows, cols), f32),
             pltpu.VMEM((rows, cols), jnp.int32),
-            pltpu.VMEM((rows, rank, cols), f32),
             pltpu.VMEM((rows, rank, cols), f32),
             pltpu.VMEM((2, rank, cols), f32),
             pltpu.VMEM((2, rows, cols), jnp.int32),
@@ -286,20 +297,33 @@
             pltpu.VMEM((group, 24, dates), f32),
             pltpu.VMEM((groups, 24, dates), f32),
             pltpu.VMEM((rows + 2, cols), f32),
-            dma((steps,)), dma((steps,)), dma((rows,)), dma((2,)), dma((steps,)), dma((rows,)),
+            dma((steps,)), dma((steps,)), dma((rows,)), dma((5,)),
             dma((4,)), dma((4,)),
             dma((group,)), dma((group,)), dma((groups,)), dma((groups,)),
         ],
         compiler_params=pltpu.CompilerParams(
-            collective_id=0, has_side_effects=True, vmem_limit_bytes=40 * MIB
+            collective_id=0, has_side_effects=True, vmem_limit_bytes=GRANT
         ),
         name="gap_fill",
     )(
-        conductance, observed, weights, pixel_factors, pixel_bias, date_factors,
-        date_bias.reshape(1, dates), land_class,
-    )
-    scale = scale[0, 0]
-    return scale * u + s, scale * g, gdf, gdb.reshape(dates)
+        *(
+            pltpu.with_memory_space_constraint(x, pltpu.HBM)
+            for x in (
+                conductance, observed, weights, pixel_factors, pixel_bias, date_factors,
+                date_bias.reshape(1, dates), land_class,
+            )
+        )
+    )
+    gpf, gpb, gdf, gdb = pl.pallas_call(
+        place,
+        out_shape=shapes,
+        in_specs=[vmem] * 4,
+        out_specs=(anywhere,) * 4,
+        scratch_shapes=[dma((4,))],
+        compiler_params=pltpu.CompilerParams(vmem_limit_bytes=4 * 1024 * 1024),
+        name="place",
+    )(*grads)
+    return gpf, gpb, gdf, gdb.reshape(dates)
 
 
 def solution(mesh):

time: 38.2 us -> 26.3 us (0.69)
  local copies, waits for them, and re-layouts: 10.9 us -> 0 us
  other arithmetic: 3.01 us -> 0 us
  Pallas kernels: 23.3 us -> 25.5 us
    unnamed x18 -> x0, local copies, waits for them, and re-layouts: 10.4 us -> none
    pallas_call x1 -> x2, Pallas kernels: 23.3 us -> 25.5 us  [the longest x1 24.5 us: on_device(): pl.pallas_call(functools.partial(kernel, n, group, chunk), out_shape=tupl...]
    add x1 -> x0, other arithmetic: 1.72 us -> none  [on_device(): return (scale * u + s, scale * g, gdf, gdb.reshape(dates))]
    mul x1 -> x0, other arithmetic: 1.29 us -> none  [on_device(): return (scale * u + s, scale * g, gdf, gdb.reshape(dates))]
    slice x1 -> x0, local copies, waits for them, and re-layouts: 0.51 us -> none  [on_device(): scale = scale[0, 0]]
where the time goes in v2:
time: 26.3 us; the launch traced here: 26.1 us
  Pallas kernels  25.5 us (97%)
  between operations  0.64 us (2%)
    pallas_call x1, Pallas kernels, on_device(): pl.pallas_call(functools.partial(kernel, n, group, chunk), out_shape=tupl...  24.5 us
    pallas_call x1, Pallas kernels, on_device(): pl.pallas_call(place, out_shape=shapes, in_specs=[vmem] * 4, out_specs=(a...  1.02 us

profile of v2, /device:TPU:0, one launch (start us, length us, event | category | flops | bytes accessed | tf_op | source)
XLA Modules:
  0.0 26.1 jit_solution(17381352690970885677)
XLA Ops:
  0.6 24.5 %gap_fill.1 = (f32[4,16,4096]{2,1,0:T(8,128)S(1)}, f32[4,4096]{1,0:T(4,128)S(1)}, f32[16,128]{1,0:T(8,128)S(1)}, f32[1,128]{1,0:T(1,128)S(1)}) custom-call(f32[4]{0:T(128)} %cond_hbm.1, bf16[4,4096,128]{2,1,0:T(8,128)(2,1)} %obs_hbm.1, bf16[4,4096,128]{2,1,0:T(8,128)(2,1)} %wts_hbm.1, f32[4,16,4096]{2,1,0:T(8,128)} %fac_hbm.1, f32[4,4096]{1,0:T(4,128)} %pb_hbm.1, ...), custom_call_target="tpu_custom_call" | custom-call | tf_op jit(solution)/shard_map/gap_fill/pallas_call | solution.py:278
  25.1 1.0 %place.1 = (f32[4,16,4096]{2,1,0:T(8,128)}, f32[4,4096]{1,0:T(4,128)}, f32[16,128]{1,0:T(8,128)}, f32[1,128]{1,0:T(1,128)}) custom-call(f32[4,16,4096]{2,1,0:T(8,128)S(1)} %get-tuple-element.12.refs_0_, f32[4,4096]{1,0:T(4,128)S(1)} %get-tuple-element.13.refs_1_, f32[16,128]{1,0:T(8,128)S(1)} %get-tuple-element.14.refs_2_, ...), custom_call_target="tpu_custom_call" | custom-call | tf_op jit(solution)/shard_map/place/pallas_call | solution.py:317

commit v3 on v2

--- a/solution.py
+++ b/solution.py
@@ -8,7 +8,7 @@
 from jax.sharding import PartitionSpec as P
 
 CLASSES = 4
-CHUNK = 1024
+CHUNK = 4096
 GRANT = 44 * 1024 * 1024
 
 
@@ -37,7 +37,7 @@
     cond_hbm, obs_hbm, wts_hbm, fac_hbm, pb_hbm, df_hbm, db_hbm, lc_hbm,
     gpf_ref, gpb_ref, gdf_ref, gdb_ref,
     cond_ref, df_ref, db_ref,
-    obs, wts, fac, pb, lc, smooth, halo_f, halo_c, rhs, back, stage_a, stage_b, cond,
+    obs, wts, fac, pb, lc, smooth, halo_f, halo_c, edge_c, rhs, back, stage_a, stage_b, cond,
     obs_sem, wts_sem, fac_sem, small_sem,
     halo_send, halo_recv, a_send, a_recv, b_send, b_recv,
 ):
@@ -45,7 +45,6 @@
     dates = obs.shape[2]
     per_row = cols // chunk
     steps = rows * per_row
-    half = chunk // 2
     groups = n // group
     f32, bf16 = jnp.float32, jnp.bfloat16
 
@@ -127,54 +126,64 @@
     halo = [
         remote(fac_hbm.at[0], halo_f.at[1], halo_send.at[0], halo_recv.at[0], above),
         remote(fac_hbm.at[rows - 1], halo_f.at[0], halo_send.at[1], halo_recv.at[1], below),
-        remote(lc_hbm, halo_c.at[1], halo_send.at[2], halo_recv.at[2], above),
-        remote(lc_hbm, halo_c.at[0], halo_send.at[3], halo_recv.at[3], below),
-    ]
-    for copy in halo:
+        remote(edge_c.at[0], halo_c.at[1], halo_send.at[2], halo_recv.at[2], above),
+        remote(edge_c.at[1], halo_c.at[0], halo_send.at[3], halo_recv.at[3], below),
+    ]
+    for copy in halo[:2]:
         copy.start()
     pb_copy.wait()
 
     slot = lax.broadcasted_iota(jnp.int32, (16, chunk), 0)
 
-    def body(y, c, carry):
-        total, count = carry
-        step = y * per_row + c
-        for copy in chunk_copies(y, c, step):
-            copy.wait()
-        start = pl.multiple_of(c * chunk, chunk)
-        fh, fl = split(fac[y, :, pl.ds(start, chunk)])
-        ph, plow = split(pb[pl.ds(y, 1), pl.ds(start, chunk)])
+    def operand(y, at):
+        fh, fl = split(fac[y, :, at])
+        ph, plow = split(pb[y : y + 1, at])
         extra = jnp.where(
             slot == 0, ph.astype(f32),
             jnp.where(slot == 1, plow.astype(f32), jnp.where(slot < 4, 1.0, 0.0)),
         ).astype(bf16)
-        lhs = jnp.concatenate([fh, fl, fh, extra], axis=0)
-        halves = [lhs[:, :half], lhs[:, half:]]
+        return jnp.concatenate([fh, fl, fh, extra], axis=0)
+
+    def body(pair, c, carry):
+        total, count = carry
+        for y in pair:
+            for copy in chunk_copies(y, c, y * per_row + c):
+                copy.wait()
+        at = pl.ds(pl.multiple_of(c * chunk, chunk), chunk)
+        lhs = [operand(y, at) for y in pair]
         pred = lax.dot_general(
-            jnp.concatenate(halves, axis=0), rhs[...], (((0,), (0,)), ((), ())),
+            jnp.concatenate(lhs, axis=0), rhs[...], (((0,), (0,)), ((), ())),
             preferred_element_type=f32,
         )
-        for j in range(2):
-            at = pl.ds(pl.multiple_of(start + j * half, half), half)
+        for j, y in enumerate(pair):
             w = wts[y, at, :].astype(f32)
-            count = count + jnp.sum(w.reshape(half // 8, 8, dates), axis=0)
+            count = count + jnp.sum(w.reshape(chunk // 8, 8, dates), axis=0)
             misfit = w * (pred[:, j * dates : (j + 1) * dates] - obs[y, at, :].astype(f32))
             mh, ml = split(misfit)
             both = jnp.concatenate([mh, ml], axis=1)
             total = total + lax.dot_general(
-                halves[j], both, (((1,), (0,)), ((), ())), preferred_element_type=f32
+                lhs[j], both, (((1,), (0,)), ((), ())), preferred_element_type=f32
             )
             pix = lax.dot_general(
                 back[...], both, (((1,), (1,)), ((), ())), preferred_element_type=f32
             )
             gpf_ref[y, :, at] = pix[:rank] + pix[rank : 2 * rank]
-            gpb_ref[pl.ds(y, 1), at] = pix[2 * rank : 2 * rank + 1]
+            gpb_ref[y : y + 1, at] = pix[2 * rank : 2 * rank + 1]
         return total, count
 
     carry = (jnp.zeros((64, 2 * dates), f32), jnp.zeros((8, dates), f32))
-    for y in range(rows):
+    for y in range(0, rows, 2):
         fac_copies[y].wait()
-        carry = lax.fori_loop(0, per_row, functools.partial(body, y), carry)
+        fac_copies[y + 1].wait()
+        carry = lax.fori_loop(0, per_row, functools.partial(body, (y, y + 1)), carry)
+        if y == 0:
+            lc_copy.wait()
+            cond_copy.wait()
+            cond[1 : rows + 1] = lookup(lc[...], cond_ref)
+            edge_c[0] = cond[1:2]
+            edge_c[1] = cond[rows : rows + 1]
+            for copy in halo[2:]:
+                copy.start()
     total, count = carry
 
     gdf = total[:rank, :dates] + total[:rank, dates:] + total[rank : 2 * rank, :dates]
@@ -191,13 +200,10 @@
     for copy in sends_a:
         copy.start()
 
-    lc_copy.wait()
-    cond_copy.wait()
     for copy in halo:
         copy.wait()
-    cond[0:1] = jnp.where(me == 0, 0.0, lookup(halo_c[0, rows - 1 : rows, :], cond_ref))
-    cond[rows + 1 : rows + 2] = jnp.where(me == n - 1, 0.0, lookup(halo_c[1, 0:1, :], cond_ref))
-    cond[1 : rows + 1] = lookup(lc[...], cond_ref)
+    cond[0:1] = jnp.where(me == 0, 0.0, halo_c[0])
+    cond[rows + 1 : rows + 2] = jnp.where(me == n - 1, 0.0, halo_c[1])
 
     def row_factors(y):
         return halo_f[0] if y < 0 else halo_f[1] if y == rows else fac[y]
@@ -291,7 +297,8 @@
             pltpu.VMEM((rows, cols), jnp.int32),
             pltpu.VMEM((rows, rank, cols), f32),
             pltpu.VMEM((2, rank, cols), f32),
-            pltpu.VMEM((2, rows, cols), jnp.int32),
+            pltpu.VMEM((2, 1, cols), f32),
+            pltpu.VMEM((2, 1, cols), f32),
             pltpu.VMEM((128, 2 * dates), bf16),
             pltpu.VMEM((48, 2 * dates), bf16),
             pltpu.VMEM((group, 24, dates), f32),

time: 26.3 us -> 20 us (0.76)
  Pallas kernels: 25.5 us -> 19.2 us
    pallas_call x1, Pallas kernels: 24.5 us -> 18.2 us  [on_device(): pl.pallas_call(functools.partial(kernel, n, group, chunk), out_shape=tupl...]
where the time goes in v3:
time: 20 us; the launch traced here: 19.8 us
  Pallas kernels  19.2 us (96%)
  between operations  0.64 us (3%)
    pallas_call x1, Pallas kernels, on_device(): pl.pallas_call(functools.partial(kernel, n, group, chunk), out_shape=tupl...  18.2 us
    pallas_call x1, Pallas kernels, on_device(): pl.pallas_call(place, out_shape=shapes, in_specs=[vmem] * 4, out_specs=(a...  1.02 us

profile of v3, /device:TPU:0, one launch (start us, length us, event | category | flops | bytes accessed | tf_op | source)
XLA Modules:
  0.0 19.8 jit_solution(9357177743803697658)
XLA Ops:
  0.6 18.2 %gap_fill.1 = (f32[4,16,4096]{2,1,0:T(8,128)S(1)}, f32[4,4096]{1,0:T(4,128)S(1)}, f32[16,128]{1,0:T(8,128)S(1)}, f32[1,128]{1,0:T(1,128)S(1)}) custom-call(f32[4]{0:T(128)} %cond_hbm.1, bf16[4,4096,128]{2,1,0:T(8,128)(2,1)} %obs_hbm.1, bf16[4,4096,128]{2,1,0:T(8,128)(2,1)} %wts_hbm.1, f32[4,16,4096]{2,1,0:T(8,128)} %fac_hbm.1, f32[4,4096]{1,0:T(4,128)} %pb_hbm.1, ...), custom_call_target="tpu_custom_call" | custom-call | tf_op jit(solution)/shard_map/gap_fill/pallas_call | solution.py:284
  18.8 1.0 %place.1 = (f32[4,16,4096]{2,1,0:T(8,128)}, f32[4,4096]{1,0:T(4,128)}, f32[16,128]{1,0:T(8,128)}, f32[1,128]{1,0:T(1,128)}) custom-call(f32[4,16,4096]{2,1,0:T(8,128)S(1)} %get-tuple-element.12.refs_0_, f32[4,4096]{1,0:T(4,128)S(1)} %get-tuple-element.13.refs_1_, f32[16,128]{1,0:T(8,128)S(1)} %get-tuple-element.14.refs_2_, ...), custom_call_target="tpu_custom_call" | custom-call | tf_op jit(solution)/shard_map/place/pallas_call | solution.py:324
